TPU v7x, 256 devices: a whole 4x4x8 slice. The times are simulated.
256 devices in a mesh: strike: 64 (over y, z, core), dip: 4 (over x).
Axes of the slice: x: 4, y: 4, z: 8, core: 2. Of those that a mesh axis runs over, the one named last changes fastest.
Arguments:
- slip_rate: float32 [3, 4096, 1024], P(None, 'strike', 'dip'), may hold values from -6 to 6
- history: bfloat16 [4, 3, 2, 1024, 4096], P(None, None, None, ('strike', 'dip')), may hold values from -6 to 6
- lengths: int32 [1024, 4096], P(('strike', 'dip')), may hold values from 1 to 4, as said below
- prestress: float32 [2, 4096, 1024], P(None, 'strike', 'dip'), may hold values from -8 to 8
- normal_stress: float32 [4096, 1024], P('strike', 'dip'), may hold values from 8 to 16
- direct_effect: float32 [4096, 1024], P('strike', 'dip'), may hold values from 0.01 to 0.04
- state_log: float32 [4096, 1024], P('strike', 'dip'), may hold values from 1 to 5
Outputs:
- next_rates: float32 [3, 4096, 1024], P(None, 'strike', 'dip')
- next_state: float32 [4096, 1024], P('strike', 'dip')
Inputs may be any that keep to these rules, and one draw needn't show every extreme that they name: `lengths`: how many of the newest slip-rate spectra enter each wavenumber's stress transfer.
All inputs are finite; a program needn't handle non-finite values.
Results may differ from a plain program's by a relative error of at most 0.0003.
Values sent between devices are 32-bit elements; how exact they have to be, the bound alone decides.
No kernel may reach another device: no remote copies, remote signals or barrier semaphores. Data moves between devices by JAX's collectives and lax.ppermute only.
A program may use at most 128 MiB of HBM per device.

v0:
```python
import math
import jax
import jax.numpy as jnp
from jax import lax
from jax.sharding import PartitionSpec as P

HIST = 4
NEWTON = 2
time_step = 0.5
coupling = 0.5
decay_rate = 0.05
shear_speed = 0.6
opening_speed = 1.7
radiation = 0.5
healing = 1.0
slip_length = 2.0
highest = lax.Precision.HIGHEST


def area_sine(ratio):
    return jnp.log(ratio + jnp.sqrt(ratio * ratio + 1.0))


def wave_geometry(dip_modes, strike_modes, dip_cells, strike_cells):
    signed_dip = jnp.where(2 * dip_modes < dip_cells, dip_modes, dip_modes - dip_cells)
    signed_strike = jnp.where(
        2 * strike_modes < strike_cells, strike_modes, strike_modes - strike_cells
    )
    wave_dip = signed_dip.astype(jnp.float32) * (2.0 * math.pi / dip_cells)
    wave_strike = signed_strike.astype(jnp.float32) * (2.0 * math.pi / strike_cells)
    modulus = jnp.sqrt(wave_strike * wave_strike + wave_dip * wave_dip)
    anchor = (signed_dip == 0) & (signed_strike == 0)
    safe_modulus = jnp.where(anchor, 1.0, modulus)
    unit_strike = jnp.where(anchor, 1.0, wave_strike / safe_modulus)
    unit_dip = jnp.where(anchor, 0.0, wave_dip / safe_modulus)
    return (modulus, unit_strike, unit_dip)


def delay_mixing(geometry, delay):
    modulus, unit_strike, unit_dip = geometry
    phase_arg = modulus * (time_step * (delay + 1.0))
    envelope = -coupling * time_step * modulus * jnp.exp(-decay_rate * phase_arg)
    mode_two = envelope * jnp.cos(phase_arg)
    mode_three = envelope * jnp.cos(shear_speed * phase_arg)
    mode_one = envelope * jnp.cos(opening_speed * phase_arg)
    mix_along = unit_strike * unit_strike * mode_two + unit_dip * unit_dip * mode_three
    mix_cross = unit_strike * unit_dip * (mode_two - mode_three)
    mix_across = unit_dip * unit_dip * mode_two + unit_strike * unit_strike * mode_three
    return (mix_along, mix_cross, mix_across, mode_one)


def delay_term(spectrum, mixing, active):
    mix_along, mix_cross, mix_across, mode_one = mixing
    force_strike = (mix_along * spectrum[0] + mix_cross * spectrum[1]) * active
    force_dip = (mix_cross * spectrum[0] + mix_across * spectrum[1]) * active
    force_open = mode_one * spectrum[2] * active
    return jnp.stack([force_strike, force_dip, force_open])


def friction_step(force_field, prestress, normal_stress, direct_effect, state_log):
    load_strike = prestress[0] + force_field[0]
    load_dip = prestress[1] + force_field[1]
    traction = jnp.sqrt(load_strike * load_strike + load_dip * load_dip)
    strength = direct_effect * normal_stress
    factor = 2.0 * radiation * jnp.exp(-state_log)
    estimate = jnp.minimum(traction / strength, area_sine(traction / factor))
    for repeat in range(NEWTON):
        residual = traction - strength * estimate - factor * jnp.sinh(estimate)
        estimate = estimate + residual / (strength + factor * jnp.cosh(estimate))
    slip_speed = (traction - strength * estimate) / radiation
    unit_scale = slip_speed / jnp.maximum(traction, 1.0)
    new_rates = jnp.stack(
        [unit_scale * load_strike, unit_scale * load_dip, force_field[2] / radiation]
    )
    new_state = state_log + time_step * (healing * jnp.exp(-state_log) - slip_speed / slip_length)
    return (new_rates, new_state)


def phase_table(first_index, second_index, period):
    turn_count = first_index[:, None] * second_index[None, :] % period
    angle_table = turn_count.astype(jnp.float32) * (2.0 * math.pi / period)
    return (jnp.cos(angle_table), jnp.sin(angle_table))


def contract(pattern, first_operand, second_operand):
    return jnp.einsum(pattern, first_operand, second_operand, precision=highest)


def pair_section(part_real, part_imag, pattern, cos_table, sin_table, sign):
    out_real = contract(pattern, part_real, cos_table) - sign * contract(
        pattern, part_imag, sin_table
    )
    out_imag = contract(pattern, part_imag, cos_table) + sign * contract(
        pattern, part_real, sin_table
    )
    return (out_real, out_imag)


def twist_phase(part_real, part_imag, cos_table, sin_table, sign):
    out_real = cos_table * part_real - sign * sin_table * part_imag
    out_imag = cos_table * part_imag + sign * sin_table * part_real
    return (out_real, out_imag)


def shards(slip_rate, history, lengths, prestress, normal_stress, direct_effect, state_log):
    strike_count = lax.axis_size("strike")
    dip_count = lax.axis_size("dip")
    strike_index = lax.axis_index("strike")
    dip_index = lax.axis_index("dip")
    row_count = slip_rate.shape[1]
    dip_block = slip_rate.shape[2]
    mode_rows = history.shape[3]
    strike_cells = history.shape[4]
    dip_cells = dip_block * dip_count
    unit_modes = dip_count * mode_rows
    norm_dip = 1.0 / math.sqrt(dip_cells)
    norm_strike = 1.0 / math.sqrt(strike_cells)
    local_modes = jnp.arange(mode_rows, dtype=jnp.int32)
    dip_modes = (strike_index * dip_count + dip_index) * mode_rows + local_modes
    strike_modes = jnp.arange(strike_cells, dtype=jnp.int32)
    geometry = wave_geometry(dip_modes[:, None], strike_modes[None, :], dip_cells, strike_cells)
    coarse_all = jnp.arange(unit_modes, dtype=jnp.int32)
    coarse_own = dip_index * mode_rows + local_modes
    outer_index = jnp.arange(strike_count, dtype=jnp.int32)
    inner_index = jnp.arange(row_count, dtype=jnp.int32)
    cos_outer, sin_outer = phase_table(outer_index, outer_index, strike_count)
    cos_bend, sin_bend = phase_table(outer_index, inner_index, strike_cells)
    cos_bend = cos_bend * norm_strike
    sin_bend = sin_bend * norm_strike
    cos_inner, sin_inner = phase_table(inner_index, inner_index, row_count)

    def strike_forward(spectral):
        item_count = spectral.shape[0]
        grid_view = spectral.reshape(item_count, 2, mode_rows, strike_count, row_count)
        section_real, section_imag = pair_section(
            grid_view[:, 0], grid_view[:, 1], "ngpr,kp->ngkr", cos_outer, sin_outer, -1.0
        )
        bent_real, bent_imag = twist_phase(section_real, section_imag, cos_bend, sin_bend, -1.0)
        out_real, out_imag = pair_section(
            bent_real, bent_imag, "ngkr,rm->ngmk", cos_inner, sin_inner, -1.0
        )
        return jnp.stack([out_real, out_imag], axis=1).reshape(
            item_count, 2, mode_rows, strike_cells
        )

    def strike_inverse(spectral):
        grid_view = spectral.reshape(3, 2, mode_rows, row_count, strike_count)
        section_real, section_imag = pair_section(
            grid_view[:, 0], grid_view[:, 1], "ngmk,rm->ngrk", cos_inner, sin_inner, 1.0
        )
        bent_real, bent_imag = twist_phase(section_real, section_imag, cos_bend.T, sin_bend.T, 1.0)
        out_real, out_imag = pair_section(
            bent_real, bent_imag, "ngrk,kp->ngpr", cos_outer, sin_outer, 1.0
        )
        return jnp.stack([out_real, out_imag], axis=1).reshape(3, 2, mode_rows, strike_cells)

    def to_modes(space_field):
        gathered = lax.all_gather(space_field, "dip", axis=2, tiled=True)
        cos_first, sin_first = phase_table(coarse_all, coarse_own, unit_modes)
        cos_twist, sin_twist = phase_table(outer_index, coarse_own, dip_cells)
        grid_view = gathered.reshape(3, row_count, unit_modes, strike_count)
        first_real = contract("cxab,au->cxbu", grid_view, cos_first)
        first_imag = -contract("cxab,au->cxbu", grid_view, sin_first)
        bent_real, bent_imag = twist_phase(
            first_real, first_imag, cos_twist * norm_dip, sin_twist * norm_dip, -1.0
        )
        out_real, out_imag = pair_section(
            bent_real, bent_imag, "cxbi,bs->csix", cos_outer, sin_outer, -1.0
        )
        dip_spec = jnp.stack([out_real, out_imag], axis=1).reshape(3, 2, dip_block, row_count)
        return strike_forward(
            lax.all_to_all(dip_spec, "strike", split_axis=2, concat_axis=3, tiled=True)
        )

    def to_space(mode_field):
        mixed_rows = strike_inverse(mode_field)
        dip_spec = lax.all_to_all(mixed_rows, "strike", split_axis=3, concat_axis=2, tiled=True)
        gathered = lax.all_gather(dip_spec, "dip", axis=2, tiled=True)
        grid_view = gathered.reshape(3, 2, dip_count, strike_count, mode_rows, row_count)
        cos_last, sin_last = phase_table(coarse_own, coarse_all, unit_modes)
        first_real, first_imag = pair_section(
            grid_view[:, 0], grid_view[:, 1], "cdsix,bs->cxbdi", cos_outer, sin_outer, 1.0
        )
        first_real = first_real.reshape(3, row_count, strike_count, unit_modes)
        first_imag = first_imag.reshape(3, row_count, strike_count, unit_modes)
        cos_twist, sin_twist = phase_table(outer_index, coarse_all, dip_cells)
        bent_real, bent_imag = twist_phase(
            first_real, first_imag, cos_twist * norm_dip, sin_twist * norm_dip, 1.0
        )
        space_part = contract("cxbu,au->cxab", bent_real, cos_last) - contract(
            "cxbu,au->cxab", bent_imag, sin_last
        )
        return space_part.reshape(3, row_count, dip_block)

    def transfer(recent):
        recent_count = len(recent)
        summed = jnp.zeros(recent[0].shape, jnp.float32)
        for offset in range(HIST):
            if offset < recent_count:
                source = recent[offset]
            else:
                source = history[offset - recent_count].astype(jnp.float32)
            active = (offset < lengths).astype(jnp.float32)
            summed = summed + delay_term(source, delay_mixing(geometry, float(offset)), active)
        return summed

    first_spec = to_modes(slip_rate)
    force_field = to_space(transfer([first_spec]))
    next_rates, next_state = friction_step(
        force_field, prestress, normal_stress, direct_effect, state_log
    )
    second_spec = to_modes(next_rates)
    force_field = to_space(transfer([second_spec, first_spec]))
    next_rates, next_state = friction_step(
        force_field, prestress, normal_stress, direct_effect, next_state
    )
    return (next_rates, next_state)


def solution(mesh):
    return jax.shard_map(
        shards,
        mesh=mesh,
        in_specs=(
            P(None, "strike", "dip"),
            P(None, None, None, ("strike", "dip"), None),
            P(("strike", "dip"), None),
            P(None, "strike", "dip"),
            P("strike", "dip"),
            P("strike", "dip"),
            P("strike", "dip"),
        ),
        out_specs=(P(None, "strike", "dip"), P("strike", "dip")),
        check_vma=False,
    )
```

profile of v0, /device:TPU:1, one launch (start us, length us, event | category | flops | bytes accessed | tf_op | source)
XLA Modules:
  0.0 520.3 jit_solution(6019969516380714102)
XLA Ops:
  7.3 13.1 %all_gather.12 = f32[3,64,1024]{2,1,0:T(8,128)S(1)} all-gather(f32[3,64,256]{2,1,0:T(8,128)} %param.7), channel_id=1, replica_groups=mesh['strike'=64,'dip'=4] {'dip'}, dimensions={2}, use_global_device_ids=true | all-gather | bytes 983040 | tf_op jit(solution)/shard_map/all_gather | solution.py:158
  31.2 13.9 %all-to-all-start = ((f32[64,1,1536]{2,1,0:T(1,128)}), f32[64,1,1536]{2,1,0:T(1,128)S(1)}, u32[]{:S(2)}, u32[]{:S(2)}) async-start(f32[64,1,1536]{2,1,0:T(1,128)} %reshape.1792), calls=%async_computation | async-start | bytes 786432 | tf_op jit(solution)/shard_map/all_to_all | solution.py:172
  45.9 4.1 multiply_add_fusion.20
  60.7 2.8 multiply_add_fusion.5
  84.6 10.5 %copy.366 = f32[3,1,4,4096]{2,1,0,3:T(1,128)} copy(f32[3,1,4,4096]{3,2,0,1:T(4,128)S(1)} %stack.171) | data formatting | bytes 393216 | tf_op jit(solution)/shard_map/stack | solution.py:155
  96.7 10.3 %copy.367 = f32[3,1,4,4096]{2,1,0,3:T(1,128)} copy(f32[3,1,4,4096]{3,2,0,1:T(4,128)S(1)} %stack.172) | data formatting | bytes 393216 | tf_op jit(solution)/shard_map/stack | solution.py:155
  107.0 16.7 %fusion.506 = f32[4096,3,2,4]{3,2,1,0:T(2,128)} fusion(f32[3,1,4,4096]{2,1,0,3:T(1,128)} %copy.367, f32[3,1,4,4096]{2,1,0,3:T(1,128)} %copy.366), kind=kLoop, calls=%fused_computation.664 | loop fusion | flops 98304 | bytes 786432
  123.7 16.7 %reshape.1794 = f32[64,1,1536]{2,1,0:T(1,128)S(1)} reshape(f32[4096,3,2,4]{3,2,1,0:T(2,128)} %fusion.506) | data formatting | bytes 786432
  140.4 24.7 %all_to_all.66 = f32[64,1,1536]{2,1,0:T(1,128)S(1)} all-to-all(f32[64,1,1536]{2,1,0:T(1,128)S(1)} %reshape.1794), channel_id=1, replica_groups=mesh['strike'=64,'dip'=4] {'strike'}, dimensions={0} | all-to-all | bytes 786432 | tf_op jit(solution)/shard_map/all_to_all | solution.py:177
  166.7 21.1 %reshape.1795 = f32[4096,3,2,4]{3,2,1,0:T(2,128)} reshape(f32[64,1536]{1,0:T(8,128)S(1)} %reduce.1) | data formatting | bytes 786432
  187.8 16.1 %copy.455 = f32[3,2,4,64,64]{4,3,2,1,0:T(8,128)S(1)} copy(f32[3,2,4,64,64]{2,1,0,4,3:T(2,128)} %bitcast.476) | data formatting | bytes 786432 | tf_op jit(solution)/shard_map/all_to_all | solution.py:177
  205.5 38.9 %all-gather.3.cloned.1.call-done = f32[3,2,1024,64]{3,2,1,0:T(8,128)} async-done(((f32[3,2,256,64]{3,2,1,0:T(8,128)}), f32[3,2,1024,64]{3,2,1,0:T(8,128)}) %all-gather.3.cloned.1.call-update) | async-done | bytes 1572880 | tf_op jit(solution)/shard_map/all_gather | solution.py:178
  244.4 2.1 fusion.502
  248.2 2.8 fusion.16
  251.0 2.8 convolution_add_fusion.1
  255.9 4.2 convolution_subtract_fusion.1
  267.3 10.6 %all_gather.14 = f32[3,64,1024]{2,1,0:T(8,128)S(1)} all-gather(f32[3,64,256]{2,1,0:T(8,128)S(1)} %pad_maximum_fusion.6), channel_id=1, replica_groups=mesh['strike'=64,'dip'=4] {'dip'}, dimensions={2}, use_global_device_ids=true | all-gather | bytes 983040 | tf_op jit(solution)/shard_map/all_gather | solution.py:158
  288.9 14.7 %all-to-all-start.2 = ((f32[64,1,1536]{2,1,0:T(1,128)}), f32[64,1,1536]{2,1,0:T(1,128)S(1)}, u32[]{:S(2)}, u32[]{:S(2)}) async-start(f32[64,1,1536]{2,1,0:T(1,128)} %reshape.1796), calls=%async_computation.2 | async-start | bytes 786432 | tf_op jit(solution)/shard_map/all_to_all | solution.py:172
  307.8 10.3 %all-to-all-done.2 = f32[64,1,1536]{2,1,0:T(1,128)S(1)} async-done(((f32[64,1,1536]{2,1,0:T(1,128)}), f32[64,1,1536]{2,1,0:T(1,128)S(1)}, u32[]{:S(2)}, u32[]{:S(2)}) %all-to-all-start.2) | async-done | bytes 393248 | tf_op jit(solution)/shard_map/all_to_all | solution.py:172
  336.6 10.3 %copy.396 = f32[3,1,4,4096]{2,1,0,3:T(1,128)} copy(f32[3,1,4,4096]{3,2,0,1:T(4,128)S(1)} %stack.193) | data formatting | bytes 393216 | tf_op jit(solution)/shard_map/stack | solution.py:155
  348.6 10.3 %copy.397 = f32[3,1,4,4096]{2,1,0,3:T(1,128)} copy(f32[3,1,4,4096]{3,2,0,1:T(4,128)S(1)} %stack.194) | data formatting | bytes 393216 | tf_op jit(solution)/shard_map/stack | solution.py:155
  358.8 16.7 %fusion.505 = f32[4096,3,2,4]{3,2,1,0:T(2,128)} fusion(f32[3,1,4,4096]{2,1,0,3:T(1,128)} %copy.397, f32[3,1,4,4096]{2,1,0,3:T(1,128)} %copy.396), kind=kLoop, calls=%fused_computation.663 | loop fusion | flops 98304 | bytes 786432
  375.5 16.7 %reshape.1798 = f32[64,1,1536]{2,1,0:T(1,128)S(1)} reshape(f32[4096,3,2,4]{3,2,1,0:T(2,128)} %fusion.505) | data formatting | bytes 786432
  392.3 20.6 %all_to_all.67 = f32[64,1,1536]{2,1,0:T(1,128)S(1)} all-to-all(f32[64,1,1536]{2,1,0:T(1,128)S(1)} %reshape.1798), channel_id=1, replica_groups=mesh['strike'=64,'dip'=4] {'strike'}, dimensions={0} | all-to-all | bytes 786432 | tf_op jit(solution)/shard_map/all_to_all | solution.py:177
  414.4 21.1 %reshape.1799 = f32[4096,3,2,4]{3,2,1,0:T(2,128)} reshape(f32[64,1536]{1,0:T(8,128)S(1)} %reduce.3) | data formatting | bytes 786432
  435.5 15.9 %copy.467 = f32[3,2,4,64,64]{4,3,2,1,0:T(8,128)S(1)} copy(f32[3,2,4,64,64]{2,1,0,4,3:T(2,128)} %bitcast.477) | data formatting | bytes 786432 | tf_op jit(solution)/shard_map/all_to_all | solution.py:177
  452.9 37.3 %all-gather.5.cloned.1.call-done = f32[3,2,1024,64]{3,2,1,0:T(8,128)} async-done(((f32[3,2,256,64]{3,2,1,0:T(8,128)}), f32[3,2,1024,64]{3,2,1,0:T(8,128)}) %all-gather.5.cloned.1.call-update) | async-done | bytes 1572880 | tf_op jit(solution)/shard_map/all_gather | solution.py:178
  490.2 2.1 fusion.501
  494.0 2.8 fusion.18
  496.8 2.8 convolution_add_fusion
  499.6 2.1 copy.403
  501.7 4.2 convolution_subtract_fusion
  (207 shorter events, 105.6 us)
Async XLA Ops:
  28.9 16.8 %copy-start.34 = (s32[4,4096]{1,0:T(4,128)S(1)}, s32[4,4096]{1,0:T(4,128)}, u32[]{:S(2)}) copy-start(s32[4,4096]{1,0:T(4,128)} %param.9) | copy-start | bytes 196612
  28.9 16.8 %copy-start.33 = (bf16[4,3,2,4,4096]{4,3,2,1,0:T(4,128)(2,1)S(1)}, bf16[4,3,2,4,4096]{4,3,2,1,0:T(4,128)(2,1)}, u32[]{:S(2)}) copy-start(bf16[4,3,2,4,4096]{4,3,2,1,0:T(4,128)(2,1)} %param.8) | copy-start | bytes 2359300
  31.2 32.3 %all-to-all-start = ((f32[64,1,1536]{2,1,0:T(1,128)}), f32[64,1,1536]{2,1,0:T(1,128)S(1)}, u32[]{:S(2)}, u32[]{:S(2)}) async-start(f32[64,1,1536]{2,1,0:T(1,128)} %reshape.1792), calls=%async_computation | async-start | bytes 786432 | tf_op jit(solution)/shard_map/all_to_all | solution.py:172
  45.1 199.3 %all-gather.3.cloned.1.call-start = ((), (), s32[]{:S(2)}) async-start(), calls=%async_computation.4 | async-start | bytes 3932160 | tf_op jit(solution)/shard_map/all_gather | solution.py:178
  63.5 11.3 %copy-start.7 = (f32[4,64,64]{2,1,0:T(8,128)}, f32[4,64,64]{2,1,0:T(8,128)S(1)}, u32[]{:S(2)}) copy-start(f32[4,64,64]{2,1,0:T(8,128)S(1)} %get-tuple-element.73) | copy-start | bytes 196612
  63.5 12.3 %copy-start.1 = (f32[4,64,64]{2,1,0:T(8,128)}, f32[4,64,64]{2,1,0:T(8,128)S(1)}, u32[]{:S(2)}) copy-start(f32[4,64,64]{2,1,0:T(8,128)S(1)} %get-tuple-element.55) | copy-start | bytes 196612
  63.5 12.3 %copy-start.3 = (f32[4,64,64]{2,1,0:T(8,128)}, f32[4,64,64]{2,1,0:T(8,128)S(1)}, u32[]{:S(2)}) copy-start(f32[4,64,64]{2,1,0:T(8,128)S(1)} %get-tuple-element.56) | copy-start | bytes 196612
  63.5 12.3 %copy-start.5 = (f32[4,64,64]{2,1,0:T(8,128)}, f32[4,64,64]{2,1,0:T(8,128)S(1)}, u32[]{:S(2)}) copy-start(f32[4,64,64]{2,1,0:T(8,128)S(1)} %get-tuple-element.58) | copy-start | bytes 196612
  74.8 1.9 copy-start.18
  75.8 1.5 copy-start.16
  75.8 1.6 copy-start.17
  263.4 1.4 copy-start
  286.6 17.2 %copy-start.29 = (f32[1,2,4,4096]{3,2,1,0:T(4,128)S(1)}, f32[1,2,4,4096]{3,2,1,0:T(4,128)}, u32[]{:S(2)}) copy-start(f32[1,2,4,4096]{3,2,1,0:T(4,128)} %get-tuple-element.48) | copy-start | bytes 393220
  287.3 16.8 %copy-start.28 = (f32[1,2,4,4096]{3,2,1,0:T(4,128)S(1)}, f32[1,2,4,4096]{3,2,1,0:T(4,128)}, u32[]{:S(2)}) copy-start(f32[1,2,4,4096]{3,2,1,0:T(4,128)} %get-tuple-element.47) | copy-start | bytes 393220
  287.3 16.9 %copy-start.27 = (f32[1,2,4,4096]{3,2,1,0:T(4,128)S(1)}, f32[1,2,4,4096]{3,2,1,0:T(4,128)}, u32[]{:S(2)}) copy-start(f32[1,2,4,4096]{3,2,1,0:T(4,128)} %get-tuple-element.46) | copy-start | bytes 393220
  287.3 17.9 %copy-start.32 = (f32[1,2,4,4096]{3,2,1,0:T(4,128)S(1)}, f32[1,2,4,4096]{3,2,1,0:T(4,128)}, u32[]{:S(2)}) copy-start(f32[1,2,4,4096]{3,2,1,0:T(4,128)} %get-tuple-element.51) | copy-start | bytes 393220
  287.3 18.7 %copy-start.31 = (f32[1,2,4,4096]{3,2,1,0:T(4,128)S(1)}, f32[1,2,4,4096]{3,2,1,0:T(4,128)}, u32[]{:S(2)}) copy-start(f32[1,2,4,4096]{3,2,1,0:T(4,128)} %get-tuple-element.50) | copy-start | bytes 393220
  288.9 18.0 %copy-start.30 = (f32[1,2,4,4096]{3,2,1,0:T(4,128)S(1)}, f32[1,2,4,4096]{3,2,1,0:T(4,128)}, u32[]{:S(2)}) copy-start(f32[1,2,4,4096]{3,2,1,0:T(4,128)} %get-tuple-element.49) | copy-start | bytes 393220
  288.9 29.2 %all-to-all-start.2 = ((f32[64,1,1536]{2,1,0:T(1,128)}), f32[64,1,1536]{2,1,0:T(1,128)S(1)}, u32[]{:S(2)}, u32[]{:S(2)}) async-start(f32[64,1,1536]{2,1,0:T(1,128)} %reshape.1796), calls=%async_computation.2 | async-start | bytes 786432 | tf_op jit(solution)/shard_map/all_to_all | solution.py:172
  303.6 186.7 %all-gather.5.cloned.1.call-start = ((), (), s32[]{:S(2)}) async-start(), calls=%async_computation.5 | async-start | bytes 3932160 | tf_op jit(solution)/shard_map/all_gather | solution.py:178
  325.7 2.9 copy-start.2
  325.7 2.9 copy-start.4
  325.7 2.9 copy-start.6
  325.7 2.9 copy-start.8
  327.2 1.7 copy-start.9
  327.2 1.7 copy-start.19
  327.2 1.7 copy-start.20
  327.2 1.7 copy-start.21
  327.2 1.7 copy-start.22
  327.2 1.7 copy-start.23
  327.2 1.7 copy-start.24
  509.2 1.4 copy-start.26
  (7 other events, 7.7 us)
Sparse Core Ops, SparseCore 0:
  205.5 38.8 all-gather.2
  453.0 37.1 all-gather.4
where the time goes:
time: 528 us; the launch traced here: 520 us
  local copies, waits for them, and re-layouts  189 us (36%)
  waiting for transfers between devices  86.6 us (16%)
  matrix products  75.4 us (14%)
  blocking collectives  69 us (13%)
  other arithmetic  56.3 us (11%)
  starting transfers between devices  29.3 us (6%)
  between operations  15.2 us (3%)
    unnamed x78, local copies, waits for them, and re-layouts  81.5 us
    all_gather x2, waiting for transfers between devices, to_space(): gathered = lax.all_gather(dip_spec, 'dip', axis=2, tiled=True)  76.3 us
    dot_general x56, matrix products, contract(): return jnp.einsum(pattern, first_operand, second_operand, precision=highest)  75.4 us
    all_to_all x2, blocking collectives, to_space(): lax.all_to_all(mixed_rows, 'strike', split_axis=3, concat_axis=2, tiled=T...  45.3 us
    another operation x8, local copies, waits for them, and re-layouts, strike_inverse(): jnp.stack([out_real, out_imag], axis=1)  42.1 us
    all_to_all x4, local copies, waits for them, and re-layouts, to_space(): lax.all_to_all(mixed_rows, 'strike', split_axis=3, concat_axis=2, tiled=T...  34.9 us
    unnamed x2, other arithmetic  33.4 us
    all_to_all x2, starting transfers between devices, to_modes(): lax.all_to_all(dip_spec, 'strike', split_axis=2, concat_axis=3, tiled=True)  28.6 us
  transfers between devices with their start and end apart: 4, of which 3 were waited for; matrix products, arithmetic and copies ran while one was open for 4% of the time, Pallas kernels for 0%

commit v1 on v0

--- a/solution.py
+++ b/solution.py
@@ -175,7 +175,8 @@
     def to_space(mode_field):
         mixed_rows = strike_inverse(mode_field)
         dip_spec = lax.all_to_all(mixed_rows, "strike", split_axis=3, concat_axis=2, tiled=True)
-        gathered = lax.all_gather(dip_spec, "dip", axis=2, tiled=True)
+        copies = jnp.concatenate([dip_spec] * lax.axis_size("dip"), axis=2)
+        gathered = lax.all_to_all(copies, "dip", 2, 2, tiled=True)
         grid_view = gathered.reshape(3, 2, dip_count, strike_count, mode_rows, row_count)
         cos_last, sin_last = phase_table(coarse_own, coarse_all, unit_modes)
         first_real, first_imag = pair_section(

time: 528 us -> 513 us (0.972)
  waiting for transfers between devices: 86.6 us -> 30.3 us
  blocking collectives: 69 us -> 94.7 us
  local copies, waits for them, and re-layouts: 189 us -> 204 us
  between operations: 15.2 us -> 1.96 us
  other arithmetic: 56.3 us -> 69.3 us
    all_gather x2 -> x0, waiting for transfers between devices: 76.3 us -> none  [to_space(): gathered = lax.all_gather(dip_spec, 'dip', axis=2, tiled=True)]
    all_to_all x0 -> x1, blocking collectives: none -> 23.9 us  [to_space(): gathered = lax.all_to_all(copies, 'dip', 2, 2, tiled=True)]
    all_to_all x0 -> x1, waiting for transfers between devices: none -> 19.9 us  [to_space(): gathered = lax.all_to_all(copies, 'dip', 2, 2, tiled=True)]
    unnamed x78 -> x82, local copies, waits for them, and re-layouts: 81.5 us -> 97.4 us
    all_to_all x0 -> x2, other arithmetic: none -> 12.6 us  [to_space(): gathered = lax.all_to_all(copies, 'dip', 2, 2, tiled=True)]
  transfers between devices with their start and end apart: 4 -> 3, of which waited for: 3 -> 2; matrix products, arithmetic and copies ran while one was open for 4% -> 4% of each run, Pallas kernels for 0% -> 0%
where the time goes in v1:
time: 513 us; the launch traced here: 504 us
  local copies, waits for them, and re-layouts  204 us (40%)
  blocking collectives  94.7 us (18%)
  matrix products  75.8 us (15%)
  other arithmetic  69.3 us (14%)
  waiting for transfers between devices  30.3 us (6%)
  starting transfers between devices  28.7 us (6%)
    unnamed x82, local copies, waits for them, and re-layouts  97.4 us
    dot_general x56, matrix products, contract(): return jnp.einsum(pattern, first_operand, second_operand, precision=highest)  75.8 us
    all_to_all x2, blocking collectives, to_space(): lax.all_to_all(mixed_rows, 'strike', split_axis=3, concat_axis=2, tiled=T...  45.9 us
    another operation x8, local copies, waits for them, and re-layouts, strike_inverse(): jnp.stack([out_real, out_imag], axis=1)  42.4 us
    unnamed x2, other arithmetic  33.5 us
    all_to_all x4, local copies, waits for them, and re-layouts, to_space(): lax.all_to_all(mixed_rows, 'strike', split_axis=3, concat_axis=2, tiled=T...  32.5 us
    all_gather x2, blocking collectives, to_modes(): gathered = lax.all_gather(space_field, 'dip', axis=2, tiled=True)  24.9 us
    all_to_all x2, starting transfers between devices, to_modes(): lax.all_to_all(dip_spec, 'strike', split_axis=2, concat_axis=3, tiled=True)  24.4 us
  transfers between devices with their start and end apart: 3, of which 2 were waited for; matrix products, arithmetic and copies ran while one was open for 4% of the time, Pallas kernels for 0%

profile of v1, /device:TPU:1, one launch (start us, length us, event | category | flops | bytes accessed | tf_op | source)
XLA Modules:
  0.0 504.4 jit_solution(6167115436566713718)
XLA Ops:
  0.8 13.1 %all_gather.6 = f32[3,64,1024]{2,1,0:T(8,128)S(1)} all-gather(f32[3,64,256]{2,1,0:T(8,128)} %param.7), channel_id=1, replica_groups=mesh['strike'=64,'dip'=4] {'dip'}, dimensions={2}, use_global_device_ids=true | all-gather | bytes 983040 | tf_op jit(solution)/shard_map/all_gather | solution.py:158
  24.6 14.1 %all-to-all-start = ((f32[64,1,1536]{2,1,0:T(1,128)}), f32[64,1,1536]{2,1,0:T(1,128)S(1)}, u32[]{:S(2)}, u32[]{:S(2)}) async-start(f32[64,1,1536]{2,1,0:T(1,128)} %reshape.1792), calls=%async_computation | async-start | bytes 786432 | tf_op jit(solution)/shard_map/all_to_all | solution.py:172
  39.0 4.1 multiply_add_fusion.20
  77.6 10.8 %copy.378 = f32[3,1,4,4096]{2,1,0,3:T(1,128)} copy(f32[3,1,4,4096]{3,2,0,1:T(4,128)S(1)} %stack.171) | data formatting | bytes 393216 | tf_op jit(solution)/shard_map/stack | solution.py:155
  89.9 10.3 %copy.379 = f32[3,1,4,4096]{2,1,0,3:T(1,128)} copy(f32[3,1,4,4096]{3,2,0,1:T(4,128)S(1)} %stack.172) | data formatting | bytes 393216 | tf_op jit(solution)/shard_map/stack | solution.py:155
  100.2 16.7 %fusion.506 = f32[4096,3,2,4]{3,2,1,0:T(2,128)} fusion(f32[3,1,4,4096]{2,1,0,3:T(1,128)} %copy.379, f32[3,1,4,4096]{2,1,0,3:T(1,128)} %copy.378), kind=kLoop, calls=%fused_computation.666 | loop fusion | flops 98304 | bytes 786432
  116.9 16.7 %reshape.1794 = f32[64,1,1536]{2,1,0:T(1,128)S(1)} reshape(f32[4096,3,2,4]{3,2,1,0:T(2,128)} %fusion.506) | data formatting | bytes 786432
  133.7 24.9 %all_to_all.76 = f32[64,1,1536]{2,1,0:T(1,128)S(1)} all-to-all(f32[64,1,1536]{2,1,0:T(1,128)S(1)} %reshape.1794), channel_id=1, replica_groups=mesh['strike'=64,'dip'=4] {'strike'}, dimensions={0} | all-to-all | bytes 786432 | tf_op jit(solution)/shard_map/all_to_all | solution.py:177
  160.1 21.1 %reshape.1795 = f32[4096,3,2,4]{3,2,1,0:T(2,128)} reshape(f32[64,1536]{1,0:T(8,128)S(1)} %reduce.1) | data formatting | bytes 786432
  181.2 15.7 %copy.471 = f32[3,2,4,64,64]{4,3,2,1,0:T(8,128)S(1)} copy(f32[3,2,4,64,64]{2,1,0,4,3:T(2,128)} %bitcast.484) | data formatting | bytes 786432 | tf_op jit(solution)/shard_map/all_to_all | solution.py:177
  200.1 4.1 reshape.1796
  204.2 4.3 all-to-all-start.2
  208.6 19.9 %all-to-all-done.2 = f32[4,1,98304]{2,1,0:T(1,128)S(1)} async-done(((f32[4,1,98304]{2,1,0:T(1,128)}), f32[4,1,98304]{2,1,0:T(1,128)S(1)}, u32[]{:S(2)}, u32[]{:S(2)}) %all-to-all-start.2) | async-done | bytes 1572896 | tf_op jit(solution)/shard_map/all_to_all | solution.py:179
  228.5 6.3 %reduce.2 = f32[4,98304]{1,0:T(4,128)} reduce(f32[4,1,98304]{2,1,0:T(1,128)S(1)} %all-to-all-done.2, f32[]{:T(128)} %broadcast.2493), dimensions={1}, to_apply=%all_to_all.61.reduce_sub_computation | reduce | bytes 3145732 | tf_op jit(solution)/shard_map/all_to_all | solution.py:179
  234.8 3.9 reshape.1797
  243.6 3.1 convolution_add_fusion.1
  248.8 4.2 convolution_subtract_fusion.1
  260.2 11.8 %all_gather.7 = f32[3,64,1024]{2,1,0:T(8,128)S(1)} all-gather(f32[3,64,256]{2,1,0:T(8,128)S(1)} %pad_maximum_fusion.8), channel_id=1, replica_groups=mesh['strike'=64,'dip'=4] {'dip'}, dimensions={2}, use_global_device_ids=true | all-gather | bytes 983040 | tf_op jit(solution)/shard_map/all_gather | solution.py:158
  283.0 10.3 %all-to-all-start.3 = ((f32[64,1,1536]{2,1,0:T(1,128)}), f32[64,1,1536]{2,1,0:T(1,128)S(1)}, u32[]{:S(2)}, u32[]{:S(2)}) async-start(f32[64,1,1536]{2,1,0:T(1,128)} %reshape.1798), calls=%async_computation.3 | async-start | bytes 786432 | tf_op jit(solution)/shard_map/all_to_all | solution.py:172
  297.3 10.4 %all-to-all-done.3 = f32[64,1,1536]{2,1,0:T(1,128)S(1)} async-done(((f32[64,1,1536]{2,1,0:T(1,128)}), f32[64,1,1536]{2,1,0:T(1,128)S(1)}, u32[]{:S(2)}, u32[]{:S(2)}) %all-to-all-start.3) | async-done | bytes 393248 | tf_op jit(solution)/shard_map/all_to_all | solution.py:172
  326.0 10.4 %copy.410 = f32[3,1,4,4096]{2,1,0,3:T(1,128)} copy(f32[3,1,4,4096]{3,2,0,1:T(4,128)S(1)} %stack.193) | data formatting | bytes 393216 | tf_op jit(solution)/shard_map/stack | solution.py:155
  338.0 10.3 %copy.411 = f32[3,1,4,4096]{2,1,0,3:T(1,128)} copy(f32[3,1,4,4096]{3,2,0,1:T(4,128)S(1)} %stack.194) | data formatting | bytes 393216 | tf_op jit(solution)/shard_map/stack | solution.py:155
  348.2 16.7 %fusion.505 = f32[4096,3,2,4]{3,2,1,0:T(2,128)} fusion(f32[3,1,4,4096]{2,1,0,3:T(1,128)} %copy.411, f32[3,1,4,4096]{2,1,0,3:T(1,128)} %copy.410), kind=kLoop, calls=%fused_computation.665 | loop fusion | flops 98304 | bytes 786432
  365.0 16.7 %reshape.1800 = f32[64,1,1536]{2,1,0:T(1,128)S(1)} reshape(f32[4096,3,2,4]{3,2,1,0:T(2,128)} %fusion.505) | data formatting | bytes 786432
  381.7 21.0 %all_to_all.77 = f32[64,1,1536]{2,1,0:T(1,128)S(1)} all-to-all(f32[64,1,1536]{2,1,0:T(1,128)S(1)} %reshape.1800), channel_id=1, replica_groups=mesh['strike'=64,'dip'=4] {'strike'}, dimensions={0} | all-to-all | bytes 786432 | tf_op jit(solution)/shard_map/all_to_all | solution.py:177
  404.2 21.1 %reshape.1801 = f32[4096,3,2,4]{3,2,1,0:T(2,128)} reshape(f32[64,1536]{1,0:T(8,128)S(1)} %reduce.4) | data formatting | bytes 786432
  425.3 15.7 %copy.483 = f32[3,2,4,64,64]{4,3,2,1,0:T(8,128)S(1)} copy(f32[3,2,4,64,64]{2,1,0,4,3:T(2,128)} %bitcast.485) | data formatting | bytes 786432 | tf_op jit(solution)/shard_map/all_to_all | solution.py:177
  444.3 4.1 reshape.1802
  448.4 23.9 %all_to_all.78 = f32[4,1,98304]{2,1,0:T(1,128)S(1)} all-to-all(f32[4,1,98304]{2,1,0:T(1,128)} %reshape.1802), channel_id=1, replica_groups=mesh['strike'=64,'dip'=4] {'dip'}, dimensions={0} | all-to-all | bytes 3145728 | tf_op jit(solution)/shard_map/all_to_all | solution.py:179
  472.3 6.3 %reduce.5 = f32[4,98304]{1,0:T(4,128)} reduce(f32[4,1,98304]{2,1,0:T(1,128)S(1)} %all_to_all.78, f32[]{:T(128)} %broadcast.2493), dimensions={1}, to_apply=%all_to_all.69.reduce_sub_computation | reduce | bytes 3145732 | tf_op jit(solution)/shard_map/all_to_all | solution.py:179
  478.6 3.9 reshape.1803
  492.6 4.2 convolution_subtract_fusion
  (216 shorter events, 122.0 us)
Async XLA Ops:
  22.4 16.4 %copy-start.34 = (s32[4,4096]{1,0:T(4,128)S(1)}, s32[4,4096]{1,0:T(4,128)}, u32[]{:S(2)}) copy-start(s32[4,4096]{1,0:T(4,128)} %param.9) | copy-start | bytes 196612
  22.4 16.5 %copy-start.33 = (bf16[4,3,2,4,4096]{4,3,2,1,0:T(4,128)(2,1)S(1)}, bf16[4,3,2,4,4096]{4,3,2,1,0:T(4,128)(2,1)}, u32[]{:S(2)}) copy-start(bf16[4,3,2,4,4096]{4,3,2,1,0:T(4,128)(2,1)} %param.8) | copy-start | bytes 2359300
  24.6 31.9 %all-to-all-start = ((f32[64,1,1536]{2,1,0:T(1,128)}), f32[64,1,1536]{2,1,0:T(1,128)S(1)}, u32[]{:S(2)}, u32[]{:S(2)}) async-start(f32[64,1,1536]{2,1,0:T(1,128)} %reshape.1792), calls=%async_computation | async-start | bytes 786432 | tf_op jit(solution)/shard_map/all_to_all | solution.py:172
  56.5 11.2 %copy-start.7 = (f32[4,64,64]{2,1,0:T(8,128)}, f32[4,64,64]{2,1,0:T(8,128)S(1)}, u32[]{:S(2)}) copy-start(f32[4,64,64]{2,1,0:T(8,128)S(1)} %get-tuple-element.73) | copy-start | bytes 196612
  56.5 12.3 %copy-start.1 = (f32[4,64,64]{2,1,0:T(8,128)}, f32[4,64,64]{2,1,0:T(8,128)S(1)}, u32[]{:S(2)}) copy-start(f32[4,64,64]{2,1,0:T(8,128)S(1)} %get-tuple-element.55) | copy-start | bytes 196612
  56.5 12.3 %copy-start.3 = (f32[4,64,64]{2,1,0:T(8,128)}, f32[4,64,64]{2,1,0:T(8,128)S(1)}, u32[]{:S(2)}) copy-start(f32[4,64,64]{2,1,0:T(8,128)S(1)} %get-tuple-element.56) | copy-start | bytes 196612
  56.5 12.3 %copy-start.5 = (f32[4,64,64]{2,1,0:T(8,128)}, f32[4,64,64]{2,1,0:T(8,128)S(1)}, u32[]{:S(2)}) copy-start(f32[4,64,64]{2,1,0:T(8,128)S(1)} %get-tuple-element.58) | copy-start | bytes 196612
  67.7 2.0 copy-start.18
  68.7 1.4 copy-start.15
  68.7 1.5 copy-start.16
  68.8 1.6 copy-start.17
  204.2 24.3 %all-to-all-start.2 = ((f32[4,1,98304]{2,1,0:T(1,128)}), f32[4,1,98304]{2,1,0:T(1,128)S(1)}, u32[]{:S(2)}, u32[]{:S(2)}) async-start(f32[4,1,98304]{2,1,0:T(1,128)} %reshape.1796), calls=%async_computation.2 | async-start | bytes 3145728 | tf_op jit(solution)/shard_map/all_to_all | solution.py:179
  256.3 1.4 copy-start
  280.8 12.6 %copy-start.29 = (f32[1,2,4,4096]{3,2,1,0:T(4,128)S(1)}, f32[1,2,4,4096]{3,2,1,0:T(4,128)}, u32[]{:S(2)}) copy-start(f32[1,2,4,4096]{3,2,1,0:T(4,128)} %get-tuple-element.48) | copy-start | bytes 393220
  281.4 12.2 %copy-start.28 = (f32[1,2,4,4096]{3,2,1,0:T(4,128)S(1)}, f32[1,2,4,4096]{3,2,1,0:T(4,128)}, u32[]{:S(2)}) copy-start(f32[1,2,4,4096]{3,2,1,0:T(4,128)} %get-tuple-element.47) | copy-start | bytes 393220
  281.4 12.4 %copy-start.27 = (f32[1,2,4,4096]{3,2,1,0:T(4,128)S(1)}, f32[1,2,4,4096]{3,2,1,0:T(4,128)}, u32[]{:S(2)}) copy-start(f32[1,2,4,4096]{3,2,1,0:T(4,128)} %get-tuple-element.46) | copy-start | bytes 393220
  281.4 13.2 %copy-start.32 = (f32[1,2,4,4096]{3,2,1,0:T(4,128)S(1)}, f32[1,2,4,4096]{3,2,1,0:T(4,128)}, u32[]{:S(2)}) copy-start(f32[1,2,4,4096]{3,2,1,0:T(4,128)} %get-tuple-element.51) | copy-start | bytes 393220
  281.4 14.1 %copy-start.31 = (f32[1,2,4,4096]{3,2,1,0:T(4,128)S(1)}, f32[1,2,4,4096]{3,2,1,0:T(4,128)}, u32[]{:S(2)}) copy-start(f32[1,2,4,4096]{3,2,1,0:T(4,128)} %get-tuple-element.50) | copy-start | bytes 393220
  283.0 13.4 %copy-start.30 = (f32[1,2,4,4096]{3,2,1,0:T(4,128)S(1)}, f32[1,2,4,4096]{3,2,1,0:T(4,128)}, u32[]{:S(2)}) copy-start(f32[1,2,4,4096]{3,2,1,0:T(4,128)} %get-tuple-element.49) | copy-start | bytes 393220
  283.0 24.7 %all-to-all-start.3 = ((f32[64,1,1536]{2,1,0:T(1,128)}), f32[64,1,1536]{2,1,0:T(1,128)S(1)}, u32[]{:S(2)}, u32[]{:S(2)}) async-start(f32[64,1,1536]{2,1,0:T(1,128)} %reshape.1798), calls=%async_computation.3 | async-start | bytes 786432 | tf_op jit(solution)/shard_map/all_to_all | solution.py:172
  315.3 2.9 copy-start.2
  315.3 2.9 copy-start.4
  315.3 2.9 copy-start.6
  315.3 2.9 copy-start.8
  316.8 1.7 copy-start.9
  316.8 1.7 copy-start.19
  316.8 1.7 copy-start.20
  316.8 1.7 copy-start.21
  316.8 1.7 copy-start.22
  316.8 1.7 copy-start.23
  316.8 1.7 copy-start.24
  500.1 1.4 copy-start.26
  (6 other events, 6.3 us)
